TPU v7x, 256 devices: a whole 4x4x8 slice. The times are simulated.
256 devices in a mesh: prow: 32 (over y, z), pcol: 8 (over x, core).
Axes of the slice: x: 4, y: 4, z: 8, core: 2. Of those that a mesh axis runs over, the one named last changes fastest.
Arguments:
- panel_rows: float32 [2, 1024, 98304], P(None, None, ('prow', 'pcol')), may hold values from -0.078125 to 0.078125
- solved: float32 [98304, 1024], P(('prow', 'pcol')), may hold values from -6 to 6
- right_side: float32 [2, 1024, 1024], P(None, 'prow', 'pcol'), may hold values from -6 to 6
- coupling: float32 [1024, 1024], P(None, 'prow'), may hold values from -0.1875 to 0.1875
- inverses: float32 [2, 1024, 1024], P(None, 'prow'), may hold values from -2 to 2, as said below
Outputs:
- panels: float32 [2, 1024, 1024], P(None, 'prow', 'pcol')
Inputs may be any that keep to these rules, and one draw needn't show every extreme that they name: `inverses`: each tile is zero above its diagonal, and its diagonal entries are positive.
All inputs are finite; a program needn't handle non-finite values.
Results may differ from a plain program's by a relative error of at most 0.000088.
Values sent between devices are 32-bit elements; how exact they have to be, the bound alone decides.
No kernel may reach another device: no remote copies, remote signals or barrier semaphores. Data moves between devices by JAX's collectives and lax.ppermute only.
A program may use at most 64 MiB of HBM per device.

v0:
```python
import jax
import jax.numpy as jnp
from jax import lax
from jax.sharding import PartitionSpec as P


def combine_old(partial_value):
    by_rows = lax.psum_scatter(partial_value, "prow", scatter_dimension=1, tiled=True)
    return lax.psum_scatter(by_rows, "pcol", scatter_dimension=2, tiled=True)


def apply_inverse(inverse_rows, residue):
    highest = lax.Precision.HIGHEST
    return jnp.dot(
        inverse_rows,
        lax.all_gather(residue, "prow", axis=0, tiled=True),
        precision=highest,
        preferred_element_type=jnp.float32,
    )


def body(panel_rows, solved, right_side, coupling, inverses):
    highest = lax.Precision.HIGHEST
    tile_rows = panel_rows.shape[1]
    solved_rows = panel_rows.shape[2]
    flat_rows = panel_rows.reshape(2 * tile_rows, solved_rows)
    partial_value = jnp.dot(
        flat_rows, solved, precision=highest, preferred_element_type=jnp.float32
    )
    partial_value = partial_value.reshape(2, tile_rows, solved.shape[1])
    reduced = combine_old(partial_value)
    first_panel = apply_inverse(inverses[0], right_side[0] - reduced[0])
    coupling_term = jnp.dot(
        coupling, first_panel, precision=highest, preferred_element_type=jnp.float32
    )
    coupling_part = lax.psum_scatter(coupling_term, "prow", scatter_dimension=0, tiled=True)
    second_rest = right_side[1] - reduced[1] - coupling_part
    second_panel = apply_inverse(inverses[1], second_rest)
    return jnp.stack([first_panel, second_panel])


def solution(mesh):
    return jax.shard_map(
        body,
        mesh=mesh,
        in_specs=(
            P(None, None, ("prow", "pcol")),
            P(("prow", "pcol"), None),
            P(None, "prow", "pcol"),
            P(None, "prow"),
            P(None, "prow", None),
        ),
        out_specs=P(None, "prow", "pcol"),
        check_vma=False,
    )
```

profile of v0, /device:TPU:2, one launch (start us, length us, event | category | flops | bytes accessed | tf_op | source)
XLA Modules:
  0.0 615.7 jit_solution(7814447639951448719)
XLA Ops:
  6.5 0.0 copy-start
  6.5 0.0 reduce-scatter.4.cloned.1.call-start
  6.5 1.9 copy-done
  8.4 16.8 %fusion = f32[2,1024,1024]{2,1,0:T(8,128)} fusion(f32[2,1024,384]{2,1,0:T(8,128)S(1)} %copy-done, f32[384,1024]{1,0:T(8,128)} %param.6), kind=kOutput, calls=%fused_computation | convolution fusion | flops 9663676416 | bytes 13107200 | tf_op jit(solution)/shard_map/dot_general | solution.py:27
  25.2 0.0 copy-start.1
  25.2 0.0 copy-start.2
  25.2 0.0 reduce-scatter.4.cloned.1.call-update
  25.2 0.0 reduce-scatter.6.cloned.1.call-start
  25.3 233.9 %reduce-scatter.4.cloned.1.call-done = f32[2,32,1024]{2,1,0:T(8,128)} async-done(((f32[2,1024,1024]{2,1,0:T(8,128)}), f32[2,32,1024]{2,1,0:T(8,128)}) %reduce-scatter.4.cloned.1.call-update) | async-done | bytes 262160 | tf_op jit(solution)/shard_map/reduce_scatter | solution.py:8
  259.2 0.0 reduce-scatter.6.cloned.1.call-update
  259.3 0.0 reduce-scatter.8.cloned.1.call-start
  259.3 31.3 %reduce-scatter.6.cloned.1.call-done = f32[2,32,128]{2,1,0:T(8,128)} async-done(((f32[2,32,1024]{2,1,0:T(8,128)}), f32[2,32,128]{2,1,0:T(8,128)}) %reduce-scatter.6.cloned.1.call-update) | async-done | bytes 32784 | tf_op jit(solution)/shard_map/reduce_scatter | solution.py:9
  290.6 0.7 slice_subtract_fusion.1
  291.4 50.4 %all-gather = f32[1,1024,128]{2,1,0:T(8,128)S(1)} all-gather(f32[1,32,128]{2,1,0:T(8,128)S(1)} %slice_subtract_fusion.1), channel_id=2, replica_groups=mesh['prow'=32,'pcol'=8] {'prow'}, dimensions={1}, use_global_device_ids=true | all-gather | bytes 540672 | tf_op jit(solution)/shard_map/all_gather | solution.py:16
  341.8 0.0 copy-done.1
  341.8 0.4 fusion.2
  342.2 0.0 copy-done.2
  342.2 1.8 convolution_bitcast_fusion
  344.0 0.0 reduce-scatter.8.cloned.1.call-update
  344.0 215.2 %reduce-scatter.8.cloned.1.call-done = f32[32,128]{1,0:T(8,128)} async-done(((f32[1024,128]{1,0:T(8,128)}), f32[32,128]{1,0:T(8,128)}) %reduce-scatter.8.cloned.1.call-update) | async-done | bytes 16400 | tf_op jit(solution)/shard_map/reduce_scatter | solution.py:36
  559.3 0.8 fusion.9
  560.0 48.1 %all_gather.7 = f32[1024,128]{1,0:T(8,128)S(1)} all-gather(f32[32,128]{1,0:T(8,128)S(1)} %fusion.9), channel_id=1, replica_groups=mesh['prow'=32,'pcol'=8] {'prow'}, dimensions={0}, use_global_device_ids=true | all-gather | bytes 540672 | tf_op jit(solution)/shard_map/all_gather | solution.py:16
  608.1 0.4 convolution_bitcast_fusion.1
  608.5 0.6 pad_maximum_fusion
Async XLA Ops:
  6.5 1.9 copy-start
  6.5 252.7 %reduce-scatter.4.cloned.1.call-start = ((), (), s32[]{:S(2)}) async-start(), calls=%async_computation.3 | async-start | bytes 8650752 | tf_op jit(solution)/shard_map/reduce_scatter | solution.py:8
  25.2 316.6 %copy-start.1 = (f32[2,32,1024]{2,1,0:T(8,128)S(1)}, f32[2,32,1024]{2,1,0:T(8,128)}, u32[]{:S(2)}) copy-start(f32[2,32,1024]{2,1,0:T(8,128)} %param.9) | copy-start | bytes 786436
  25.2 317.0 %copy-start.2 = (f32[1024,32]{0,1:T(8,128)S(1)}, f32[1024,32]{0,1:T(8,128)}, u32[]{:S(2)}) copy-start(f32[1024,32]{0,1:T(8,128)} %param.8) | copy-start | bytes 393220
  25.2 265.4 %reduce-scatter.6.cloned.1.call-start = ((), (), s32[]{:S(2)}) async-start(), calls=%async_computation.4 | async-start | bytes 294912 | tf_op jit(solution)/shard_map/reduce_scatter | solution.py:9
  259.3 300.0 %reduce-scatter.8.cloned.1.call-start = ((), (), s32[]{:S(2)}) async-start(), calls=%async_computation.5 | async-start | bytes 540672 | tf_op jit(solution)/shard_map/reduce_scatter | solution.py:36
Sparse Core Ops, SparseCore 0:
  25.4 233.8 reduce-scatter.3
  261.7 28.8 reduce-scatter.5
  344.2 215.0 reduce-scatter.7
where the time goes:
time: 616 us
  waiting for transfers between devices  481 us (78%)
  blocking collectives  98.5 us (16%)
  matrix products  19.4 us (3%)
  between operations  13.1 us (2%)
    reduce_scatter x1, waiting for transfers between devices, combine_old(): lax.psum_scatter(partial_value, 'prow', scatter_dimension=1, tiled=True)  234 us
    reduce_scatter x1, waiting for transfers between devices, body(): lax.psum_scatter(coupling_term, 'prow', scatter_dimension=0, tiled=True)  215 us
    all_gather x2, blocking collectives, apply_inverse(): lax.all_gather(residue, 'prow', axis=0, tiled=True)  98.5 us
    reduce_scatter x1, waiting for transfers between devices, combine_old(): return lax.psum_scatter(by_rows, 'pcol', scatter_dimension=2, tiled=True)  31.3 us
    dot_general x1, matrix products, body(): jnp.dot(flat_rows, solved, precision=highest, preferred_element_type=jnp....  16.8 us
  transfers between devices with their start and end apart: 3, of which 3 were waited for; matrix products, arithmetic and copies ran while one was open for 0% of the time, Pallas kernels for 0%

commit v1 on v0

--- a/solution.py
+++ b/solution.py
@@ -2,6 +2,11 @@
 import jax.numpy as jnp
 from jax import lax
 from jax.sharding import PartitionSpec as P
+
+
+def exchange_gather(x, axis, dim):
+    outgoing = jnp.stack([x] * lax.axis_size(axis))
+    return jnp.concatenate(lax.all_to_all(outgoing, axis, 0, 0), axis=dim)
 
 
 def combine_old(partial_value):
@@ -13,7 +18,7 @@
     highest = lax.Precision.HIGHEST
     return jnp.dot(
         inverse_rows,
-        lax.all_gather(residue, "prow", axis=0, tiled=True),
+        exchange_gather(residue, "prow", 0),
         precision=highest,
         preferred_element_type=jnp.float32,
     )

time: 616 us -> 564 us (0.916)
  blocking collectives: 98.5 us -> 45.2 us
    all_gather x2 -> x0, blocking collectives: 98.5 us -> none  [apply_inverse(): lax.all_gather(residue, 'prow', axis=0, tiled=True)]
    all_to_all x0 -> x2, blocking collectives: none -> 45.2 us  [exchange_gather(): return jnp.concatenate(lax.all_to_all(outgoing, axis, 0, 0), axis=dim)]
where the time goes in v1:
time: 564 us; the launch traced here: 563 us
  waiting for transfers between devices  481 us (85%)
  blocking collectives  45.2 us (8%)
  matrix products  19.4 us (3%)
  between operations  13.1 us (2%)
    reduce_scatter x1, waiting for transfers between devices, combine_old(): lax.psum_scatter(partial_value, 'prow', scatter_dimension=1, tiled=True)  234 us
    reduce_scatter x1, waiting for transfers between devices, body(): lax.psum_scatter(coupling_term, 'prow', scatter_dimension=0, tiled=True)  216 us
    all_to_all x2, blocking collectives, exchange_gather(): return jnp.concatenate(lax.all_to_all(outgoing, axis, 0, 0), axis=dim)  45.2 us
    reduce_scatter x1, waiting for transfers between devices, combine_old(): return lax.psum_scatter(by_rows, 'pcol', scatter_dimension=2, tiled=True)  31.3 us
    dot_general x1, matrix products, body(): jnp.dot(flat_rows, solved, precision=highest, preferred_element_type=jnp....  16.8 us
  transfers between devices with their start and end apart: 3, of which 3 were waited for; matrix products, arithmetic and copies ran while one was open for 0% of the time, Pallas kernels for 0%

profile of v1, /device:TPU:2, one launch (start us, length us, event | category | flops | bytes accessed | tf_op | source)
XLA Modules:
  0.0 562.8 jit_solution(39840252275019809)
XLA Ops:
  6.5 0.0 copy-start
  6.5 0.0 reduce-scatter.4.cloned.1.call-start
  6.5 1.9 copy-done
  8.4 16.8 %fusion = f32[2,1024,1024]{2,1,0:T(8,128)} fusion(f32[2,1024,384]{2,1,0:T(8,128)S(1)} %copy-done, f32[384,1024]{1,0:T(8,128)} %param.6), kind=kOutput, calls=%fused_computation | convolution fusion | flops 9663676416 | bytes 13107200 | tf_op jit(solution)/shard_map/dot_general | solution.py:32
  25.2 0.0 copy-start.1
  25.2 0.0 copy-start.2
  25.2 0.0 reduce-scatter.4.cloned.1.call-update
  25.2 0.0 reduce-scatter.6.cloned.1.call-start
  25.3 233.9 %reduce-scatter.4.cloned.1.call-done = f32[2,32,1024]{2,1,0:T(8,128)} async-done(((f32[2,1024,1024]{2,1,0:T(8,128)}), f32[2,32,1024]{2,1,0:T(8,128)}) %reduce-scatter.4.cloned.1.call-update) | async-done | bytes 262160 | tf_op jit(solution)/shard_map/reduce_scatter | solution.py:13
  259.2 0.0 reduce-scatter.6.cloned.1.call-update
  259.3 0.0 reduce-scatter.8.cloned.1.call-start
  259.3 31.3 %reduce-scatter.6.cloned.1.call-done = f32[2,32,128]{2,1,0:T(8,128)} async-done(((f32[2,32,1024]{2,1,0:T(8,128)}), f32[2,32,128]{2,1,0:T(8,128)}) %reduce-scatter.6.cloned.1.call-update) | async-done | bytes 32784 | tf_op jit(solution)/shard_map/reduce_scatter | solution.py:14
  290.6 0.7 fusion.9
  291.4 0.1 stack.13
  291.4 25.7 %all_to_all.10 = f32[32,32,128]{2,1,0:T(8,128)S(1)} all-to-all(f32[32,32,128]{2,1,0:T(8,128)S(1)} %stack.13), channel_id=1, replica_groups=mesh['prow'=32,'pcol'=8] {'prow'}, dimensions={0} | all-to-all | bytes 1048576 | tf_op jit(solution)/shard_map/all_to_all | solution.py:9
  317.1 0.0 copy-done.1
  317.1 0.4 fusion.3
  317.5 0.0 copy-done.2
  317.5 1.8 convolution_bitcast_fusion
  319.3 0.0 reduce-scatter.8.cloned.1.call-update
  319.3 215.5 %reduce-scatter.8.cloned.1.call-done = f32[32,128]{1,0:T(8,128)} async-done(((f32[1024,128]{1,0:T(8,128)}), f32[32,128]{1,0:T(8,128)}) %reduce-scatter.8.cloned.1.call-update) | async-done | bytes 16400 | tf_op jit(solution)/shard_map/reduce_scatter | solution.py:41
  534.9 0.8 fusion.8
  535.6 0.1 stack.15
  535.7 19.5 %all_to_all.11 = f32[32,32,128]{2,1,0:T(8,128)S(1)} all-to-all(f32[32,32,128]{2,1,0:T(8,128)S(1)} %stack.15), channel_id=1, replica_groups=mesh['prow'=32,'pcol'=8] {'prow'}, dimensions={0} | all-to-all | bytes 1048576 | tf_op jit(solution)/shard_map/all_to_all | solution.py:9
  555.2 0.4 convolution_bitcast_fusion.1
  555.6 0.6 pad_maximum_fusion
Async XLA Ops:
  6.5 1.9 copy-start
  6.5 252.7 %reduce-scatter.4.cloned.1.call-start = ((), (), s32[]{:S(2)}) async-start(), calls=%async_computation.5 | async-start | bytes 8650752 | tf_op jit(solution)/shard_map/reduce_scatter | solution.py:13
  25.2 291.9 %copy-start.1 = (f32[2,32,1024]{2,1,0:T(8,128)S(1)}, f32[2,32,1024]{2,1,0:T(8,128)}, u32[]{:S(2)}) copy-start(f32[2,32,1024]{2,1,0:T(8,128)} %param.9) | copy-start | bytes 786436
  25.2 292.3 %copy-start.2 = (f32[1024,32]{0,1:T(8,128)S(1)}, f32[1024,32]{0,1:T(8,128)}, u32[]{:S(2)}) copy-start(f32[1024,32]{0,1:T(8,128)} %param.8) | copy-start | bytes 393220
  25.2 265.4 %reduce-scatter.6.cloned.1.call-start = ((), (), s32[]{:S(2)}) async-start(), calls=%async_computation.6 | async-start | bytes 294912 | tf_op jit(solution)/shard_map/reduce_scatter | solution.py:14
  259.3 275.6 %reduce-scatter.8.cloned.1.call-start = ((), (), s32[]{:S(2)}) async-start(), calls=%async_computation.7 | async-start | bytes 540672 | tf_op jit(solution)/shard_map/reduce_scatter | solution.py:41
Sparse Core Ops, SparseCore 0:
  25.4 233.8 reduce-scatter.3
  261.7 28.8 reduce-scatter.5
  319.5 215.3 reduce-scatter.7
